TPU v7x, 128 devices: a whole 4x4x4 slice. The times are simulated.
128 devices in a mesh: shard: 16 (over z, x), context: 4 (over y), tensor: 2 (over core).
Axes of the slice: x: 4, y: 4, z: 4, core: 2. Of those that a mesh axis runs over, the one named last changes fastest.
Arguments:
- inputs: float32 [32, 512, 768], P('shard', 'context'), may hold values from -6 to 6
- segment_ids: int32 [32, 512], P('shard', 'context'), may hold values from 0 to 3, never falling along the last dimension, each value on 1 to 256 neighbouring positions
- projection: bfloat16 [2, 3, 768, 768], P(None, None, 'shard', 'tensor'), may hold values from -1 to 1
- head_bias: bfloat16 [2, 2, 12, 64], P(None, None, 'tensor', 'shard'), may hold values from -3 to 3
- mixing: bfloat16 [2, 768, 768], P(None, 'tensor', 'shard'), may hold values from -0.875 to 0.875
- expansion: bfloat16 [2, 768, 3072], P(None, 'shard', 'tensor'), may hold values from -0.21875 to 0.21875
- hidden_bias: bfloat16 [2, 48, 64], P(None, 'tensor', 'shard'), may hold values from -3 to 3
- contraction: bfloat16 [2, 3072, 768], P(None, 'tensor', 'shard'), may hold values from -0.109375 to 0.109375
- norm_gains: bfloat16 [2, 2, 768], P(None, None, 'shard'), may hold values from 0.3984375 to 1.59375
- offsets: bfloat16 [2, 4, 768], P(None, None, 'shard'), may hold values from -2 to 2
- cotangent: float32 [32, 512, 768], P('shard', 'context'), may hold values from -6 to 6
Outputs:
- outputs: float32 [32, 512, 768], P('shard', 'context')
- input_grad: float32 [32, 512, 768], P('shard', 'context')
- grad_projection: float32 [2, 3, 768, 768], P(None, None, 'shard', 'tensor')
- head_grad: float32 [2, 2, 12, 64], P(None, None, 'tensor', 'shard')
- grad_mixing: float32 [2, 768, 768], P(None, 'tensor', 'shard')
- grad_expansion: float32 [2, 768, 3072], P(None, 'shard', 'tensor')
- hidden_grad: float32 [2, 48, 64], P(None, 'tensor', 'shard')
- grad_contraction: float32 [2, 3072, 768], P(None, 'tensor', 'shard')
- gains_grad: float32 [2, 2, 768], P(None, None, 'shard')
- grad_offsets: float32 [2, 4, 768], P(None, None, 'shard')
Inputs may be any that keep to these rules, and one draw needn't show every extreme that they name: `segment_ids`: within a row ids never fall; every document holds 1 to 256 positions and in every row some document holds exactly 256.
All inputs are finite; a program needn't handle non-finite values.
Results may differ from a plain program's by a relative error of at most 0.033.
Values may be sent and summed in bfloat16 or wider, within the bound.
No kernel may reach another device: no remote copies, remote signals or barrier semaphores. Data moves between devices by JAX's collectives and lax.ppermute only.
A program may use at most 128 MiB of HBM per device.

v0:
```python
import jax
import jax.numpy as jnp
from jax import lax
from jax.sharding import PartitionSpec as P

HEAD = 64
EPS = 1e-05
GELU_COEF = 0.7978845608028654
GELU_CUBE = 0.044715
MASKED = -1e30


def gelu_value(preact):
    inner_arg = GELU_COEF * (preact + GELU_CUBE * preact * preact * preact)
    return 0.5 * preact * (1.0 + jnp.tanh(inner_arg))


def gelu_slope(preact):
    inner_arg = GELU_COEF * (preact + GELU_CUBE * preact * preact * preact)
    tanh_value = jnp.tanh(inner_arg)
    return 0.5 * (1.0 + tanh_value) + 0.5 * preact * (1.0 - tanh_value * tanh_value) * GELU_COEF * (
        1.0 + 3.0 * GELU_CUBE * preact * preact
    )


def norm_forward(stream):
    center = stream - jnp.mean(stream, axis=-1, keepdims=True)
    spread = lax.rsqrt(jnp.mean(center * center, axis=-1, keepdims=True) + EPS)
    return (center * spread, spread)


def norm_backward(upstream, normed, spread, gain_row):
    scaled = upstream * gain_row
    first_mean = jnp.mean(scaled, axis=-1, keepdims=True)
    second_mean = jnp.mean(scaled * normed, axis=-1, keepdims=True)
    return spread * (scaled - first_mean - normed * second_mean)


def masked_scores(query_block, key_block, visible, head_scale):
    scores = (
        jnp.einsum("rqhe,rkhe->rhqk", query_block, key_block, preferred_element_type=jnp.float32)
        * head_scale
    )
    return jnp.where(visible, scores, MASKED)


def per_device(
    inputs,
    segment_ids,
    projection,
    head_bias,
    mixing,
    expansion,
    hidden_bias,
    contraction,
    norm_gains,
    offsets,
    cotangent,
):
    layers = projection.shape[0]
    row_count, block_length, model_width = inputs.shape
    context_size = lax.axis_size("context")
    heads_here = head_bias.shape[2]
    head_scale = HEAD ** (-0.5)
    segment_half = segment_ids.astype(jnp.bfloat16)
    query_pos = lax.axis_index("context") * block_length + jnp.arange(block_length, dtype=jnp.int32)
    key_pos = jnp.arange(block_length * context_size, dtype=jnp.int32)
    stream = inputs
    kept_state = []
    for layer_index in range(layers):
        weights = (
            lax.all_gather(projection[layer_index], "shard", axis=1, tiled=True),
            lax.all_gather(head_bias[layer_index], "shard", axis=2, tiled=True),
            lax.all_gather(mixing[layer_index], "shard", axis=1, tiled=True),
            lax.all_gather(expansion[layer_index], "shard", axis=0, tiled=True),
            lax.all_gather(hidden_bias[layer_index], "shard", axis=1, tiled=True),
            lax.all_gather(contraction[layer_index], "shard", axis=1, tiled=True),
            lax.all_gather(norm_gains[layer_index], "shard", axis=1, tiled=True),
            lax.all_gather(offsets[layer_index], "shard", axis=1, tiled=True),
        )
        (
            qkv_weight,
            qkv_bias,
            out_weight,
            up_weight,
            up_bias,
            down_weight,
            gain_rows,
            offset_rows,
        ) = weights
        gain_float = gain_rows.astype(jnp.float32)
        offset_float = offset_rows.astype(jnp.float32)
        normed_one, spread_one = norm_forward(stream)
        attend_input = (normed_one * gain_float[0] + offset_float[0]).astype(jnp.bfloat16)
        projected = jnp.einsum(
            "rtd,jdc->jrtc", attend_input, qkv_weight, preferred_element_type=jnp.float32
        )
        bias_float = qkv_bias.astype(jnp.float32).reshape(2, -1)
        query_rows = (projected[0] + bias_float[0]).astype(jnp.bfloat16)
        key_rows = projected[1].astype(jnp.bfloat16)
        value_rows = (projected[2] + bias_float[1]).astype(jnp.bfloat16)
        keys_all, values_all, segments_all = (
            lax.all_gather(key_rows, "context", axis=1, tiled=True),
            lax.all_gather(value_rows, "context", axis=1, tiled=True),
            lax.all_gather(segment_half, "context", axis=1, tiled=True),
        )
        visible = (segments_all[:, None, :] == segment_half[:, :, None]) & (
            key_pos[None, None, :] <= query_pos[None, :, None]
        )
        visible = visible[:, None]
        query_block = query_rows.reshape(row_count, block_length, heads_here, HEAD)
        key_block = keys_all.reshape(row_count, -1, heads_here, HEAD)
        value_block = values_all.reshape(row_count, -1, heads_here, HEAD)
        masked = masked_scores(query_block, key_block, visible, head_scale)
        row_top = jnp.max(masked, axis=-1, keepdims=True)
        log_total = row_top + jnp.log(jnp.sum(jnp.exp(masked - row_top), axis=-1, keepdims=True))
        soft_half = jnp.exp(masked - log_total).astype(jnp.bfloat16)
        attended = (
            jnp.einsum(
                "rhqk,rkhe->rqhe", soft_half, value_block, preferred_element_type=jnp.float32
            )
            .astype(jnp.bfloat16)
            .reshape(row_count, block_length, -1)
        )
        attend_part = jnp.einsum(
            "rtc,cd->rtd", attended, out_weight, preferred_element_type=jnp.float32
        )
        middle = stream + lax.psum(attend_part, "tensor") + offset_float[2]
        normed_two, spread_two = norm_forward(middle)
        feed_input = (normed_two * gain_float[1] + offset_float[1]).astype(jnp.bfloat16)
        preact = jnp.einsum(
            "rtd,df->rtf", feed_input, up_weight, preferred_element_type=jnp.float32
        ) + up_bias.astype(jnp.float32).reshape(-1)
        activation = gelu_value(preact).astype(jnp.bfloat16)
        feed_part = jnp.einsum(
            "rtf,fd->rtd", activation, down_weight, preferred_element_type=jnp.float32
        )
        stream = middle + lax.psum(feed_part, "tensor") + offset_float[3]
        stored = ()
        kept_state.append(
            (
                stored,
                normed_one,
                spread_one,
                attend_input,
                query_block,
                key_block,
                value_block,
                visible,
                log_total,
                attended,
                normed_two,
                spread_two,
                feed_input,
                preact,
                activation,
            )
        )
    upstream = cotangent
    collected = []
    for layer_index in reversed(range(layers)):
        (
            stored,
            normed_one,
            spread_one,
            attend_input,
            query_block,
            key_block,
            value_block,
            visible,
            log_total,
            attended,
            normed_two,
            spread_two,
            feed_input,
            preact,
            activation,
        ) = kept_state[layer_index]
        current = (
            lax.all_gather(projection[layer_index], "shard", axis=1, tiled=True),
            lax.all_gather(head_bias[layer_index], "shard", axis=2, tiled=True),
            lax.all_gather(mixing[layer_index], "shard", axis=1, tiled=True),
            lax.all_gather(expansion[layer_index], "shard", axis=0, tiled=True),
            lax.all_gather(hidden_bias[layer_index], "shard", axis=1, tiled=True),
            lax.all_gather(contraction[layer_index], "shard", axis=1, tiled=True),
            lax.all_gather(norm_gains[layer_index], "shard", axis=1, tiled=True),
            lax.all_gather(offsets[layer_index], "shard", axis=1, tiled=True),
        )
        (
            qkv_weight,
            qkv_bias,
            out_weight,
            up_weight,
            up_bias,
            down_weight,
            gain_rows,
            offset_rows,
        ) = current
        gain_float = gain_rows.astype(jnp.float32)
        upstream_half = upstream.astype(jnp.bfloat16)
        contraction_part = jnp.einsum(
            "rtf,rtd->fd", activation, upstream_half, preferred_element_type=jnp.float32
        )
        offset_down = jnp.sum(upstream, axis=(0, 1))
        hidden_back = jnp.einsum(
            "rtd,fd->rtf", upstream_half, down_weight, preferred_element_type=jnp.float32
        ) * gelu_slope(preact)
        hidden_half = hidden_back.astype(jnp.bfloat16)
        hidden_part = jnp.sum(hidden_back, axis=(0, 1)).reshape(up_bias.shape)
        expansion_part = jnp.einsum(
            "rtd,rtf->df", feed_input, hidden_half, preferred_element_type=jnp.float32
        )
        feed_partial = jnp.einsum(
            "rtf,df->rtd", hidden_half, up_weight, preferred_element_type=jnp.float32
        )
        feed_back = lax.psum(feed_partial.astype(jnp.bfloat16), "tensor").astype(jnp.float32)
        gain_two = jnp.sum(feed_back * normed_two, axis=(0, 1))
        offset_two = jnp.sum(feed_back, axis=(0, 1))
        middle_back = upstream + norm_backward(feed_back, normed_two, spread_two, gain_float[1])
        middle_half = middle_back.astype(jnp.bfloat16)
        mixing_part = jnp.einsum(
            "rtc,rtd->cd", attended, middle_half, preferred_element_type=jnp.float32
        )
        offset_mix = jnp.sum(middle_back, axis=(0, 1))
        attended_back = jnp.einsum(
            "rtd,cd->rtc", middle_half, out_weight, preferred_element_type=jnp.float32
        ).astype(jnp.bfloat16)
        back_heads = attended_back.reshape(row_count, block_length, heads_here, HEAD)
        attended_heads = attended.reshape(row_count, block_length, heads_here, HEAD)
        row_delta = jnp.sum(
            back_heads.astype(jnp.float32) * attended_heads.astype(jnp.float32), axis=-1
        )
        masked = masked_scores(query_block, key_block, visible, head_scale)
        soft = jnp.exp(masked - log_total)
        soft_half = soft.astype(jnp.bfloat16)
        prob_back = jnp.einsum(
            "rqhe,rkhe->rhqk", back_heads, value_block, preferred_element_type=jnp.float32
        )
        score_back = (
            soft * (prob_back - jnp.transpose(row_delta, (0, 2, 1))[..., None]) * head_scale
        ).astype(jnp.bfloat16)
        query_back = jnp.einsum(
            "rhqk,rkhe->rqhe", score_back, key_block, preferred_element_type=jnp.float32
        ).reshape(row_count, block_length, -1)
        key_full = jnp.einsum(
            "rhqk,rqhe->rkhe", score_back, query_block, preferred_element_type=jnp.float32
        ).reshape(row_count, block_length * context_size, -1)
        value_full = jnp.einsum(
            "rhqk,rqhe->rkhe", soft_half, back_heads, preferred_element_type=jnp.float32
        ).reshape(row_count, block_length * context_size, -1)
        key_back, value_back = (
            lax.psum_scatter(
                key_full.astype(jnp.bfloat16), "context", scatter_dimension=1, tiled=True
            ).astype(jnp.float32),
            lax.psum_scatter(
                value_full.astype(jnp.bfloat16), "context", scatter_dimension=1, tiled=True
            ).astype(jnp.float32),
        )
        head_part = jnp.stack(
            [jnp.sum(query_back, axis=(0, 1)), jnp.sum(value_back, axis=(0, 1))]
        ).reshape(qkv_bias.shape)
        project_back = jnp.stack([query_back, key_back, value_back]).astype(jnp.bfloat16)
        projection_part = jnp.einsum(
            "rtd,jrtc->jdc", attend_input, project_back, preferred_element_type=jnp.float32
        )
        input_partial = jnp.einsum(
            "jrtc,jdc->rtd", project_back, qkv_weight, preferred_element_type=jnp.float32
        )
        input_back = lax.psum(input_partial.astype(jnp.bfloat16), "tensor").astype(jnp.float32)
        gain_one = jnp.sum(input_back * normed_one, axis=(0, 1))
        offset_one = jnp.sum(input_back, axis=(0, 1))
        upstream = middle_back + norm_backward(input_back, normed_one, spread_one, gain_float[0])
        grad_parts = (
            projection_part,
            head_part,
            mixing_part,
            expansion_part,
            hidden_part,
            contraction_part,
            jnp.stack([gain_one, gain_two]),
            jnp.stack([offset_one, offset_two, offset_mix, offset_down]),
        )
        collected.insert(
            0,
            (
                lax.psum(
                    lax.psum_scatter(
                        grad_parts[0].astype(jnp.bfloat16), "shard", scatter_dimension=1, tiled=True
                    ),
                    "context",
                ).astype(jnp.float32),
                lax.psum(
                    lax.psum_scatter(
                        grad_parts[1].astype(jnp.bfloat16), "shard", scatter_dimension=2, tiled=True
                    ),
                    "context",
                ).astype(jnp.float32),
                lax.psum(
                    lax.psum_scatter(
                        grad_parts[2].astype(jnp.bfloat16), "shard", scatter_dimension=1, tiled=True
                    ),
                    "context",
                ).astype(jnp.float32),
                lax.psum(
                    lax.psum_scatter(
                        grad_parts[3].astype(jnp.bfloat16), "shard", scatter_dimension=0, tiled=True
                    ),
                    "context",
                ).astype(jnp.float32),
                lax.psum(
                    lax.psum_scatter(
                        grad_parts[4].astype(jnp.bfloat16), "shard", scatter_dimension=1, tiled=True
                    ),
                    "context",
                ).astype(jnp.float32),
                lax.psum(
                    lax.psum_scatter(
                        grad_parts[5].astype(jnp.bfloat16), "shard", scatter_dimension=1, tiled=True
                    ),
                    "context",
                ).astype(jnp.float32),
                lax.psum(
                    lax.psum_scatter(
                        grad_parts[6].astype(jnp.bfloat16), "shard", scatter_dimension=1, tiled=True
                    ),
                    "context",
                ).astype(jnp.float32),
                lax.psum(
                    lax.psum_scatter(
                        grad_parts[7].astype(jnp.bfloat16), "shard", scatter_dimension=1, tiled=True
                    ),
                    "context",
                ).astype(jnp.float32),
            ),
        )
    stacked = [jnp.stack([entry[member] for entry in collected]) for member in range(8)]
    return (
        stream,
        upstream,
        stacked[0],
        stacked[1],
        stacked[2],
        stacked[3],
        stacked[4],
        stacked[5],
        stacked[6],
        stacked[7],
    )


def solution(mesh):
    in_specs = (
        P("shard", "context", None),
        P("shard", "context"),
        P(None, None, "shard", "tensor"),
        P(None, None, "tensor", "shard"),
        P(None, "tensor", "shard"),
        P(None, "shard", "tensor"),
        P(None, "tensor", "shard"),
        P(None, "tensor", "shard"),
        P(None, None, "shard"),
        P(None, None, "shard"),
        P("shard", "context", None),
    )
    out_specs = (
        P("shard", "context", None),
        P("shard", "context", None),
        P(None, None, "shard", "tensor"),
        P(None, None, "tensor", "shard"),
        P(None, "tensor", "shard"),
        P(None, "shard", "tensor"),
        P(None, "tensor", "shard"),
        P(None, "tensor", "shard"),
        P(None, None, "shard"),
        P(None, None, "shard"),
    )
    return jax.shard_map(
        per_device, mesh=mesh, in_specs=in_specs, out_specs=out_specs, check_vma=False
    )
```

profile of v0, /device:TPU:0, one launch (start us, length us, event | category | flops | bytes accessed | tf_op | source)
XLA Modules:
  0.0 1538.7 jit_solution(7133893320823804238)
XLA Ops:
  10.4 25.5 %all-gather.1 = bf16[1,4,768]{1,0,2:T(2,128)(2,1)S(1)} all-gather(bf16[1,4,48]{1,0,2:T(2,128)(2,1)S(1)} %copy.288), channel_id=3, replica_groups=mesh['shard'=16,'context'=4,'tensor'=2] {'shard'}, dimensions={2}, use_global_device_ids=true | all-gather | bytes 6528 | tf_op jit(solution)/shard_map/all_gather | solution.py:79
  37.0 23.4 %all-gather = bf16[1,2,768]{1,0,2:T(2,128)(2,1)S(1)} all-gather(bf16[1,2,48]{1,0,2:T(2,128)(2,1)S(1)} %copy.287), channel_id=2, replica_groups=mesh['shard'=16,'context'=4,'tensor'=2] {'shard'}, dimensions={2}, use_global_device_ids=true | all-gather | bytes 3264 | tf_op jit(solution)/shard_map/all_gather | solution.py:78
  93.1 23.9 %all-gather.5 = bf16[1,384,768]{1,2,0:T(8,128)(2,1)S(1)} all-gather(bf16[1,384,48]{1,2,0:T(8,128)(2,1)S(1)} %get-tuple-element.105), channel_id=7, replica_groups=mesh['shard'=16,'context'=4,'tensor'=2] {'shard'}, dimensions={2}, use_global_device_ids=true | all-gather | bytes 626688 | tf_op jit(solution)/shard_map/all_gather | solution.py:74
  201.3 47.0 %all-gather.27.cloned.1.call-done = bf16[1,768,1536]{2,1,0:T(8,128)(2,1)} async-done(((bf16[1,48,1536]{2,1,0:T(8,128)(2,1)}), bf16[1,768,1536]{2,1,0:T(8,128)(2,1)}) %all-gather.27.cloned.1.call-update) | async-done | bytes 2359312 | tf_op jit(solution)/shard_map/all_gather | solution.py:75
  250.9 45.3 %all-gather.29.cloned.1.call-done = bf16[1,1536,768]{1,2,0:T(8,128)(2,1)} async-done(((bf16[1,1536,48]{1,2,0:T(8,128)(2,1)}), bf16[1,1536,768]{1,2,0:T(8,128)(2,1)}) %all-gather.29.cloned.1.call-update) | async-done | bytes 2359312 | tf_op jit(solution)/shard_map/all_gather | solution.py:77
  300.7 23.3 %all-gather.10 = bf16[1,4,768]{1,0,2:T(2,128)(2,1)S(1)} all-gather(bf16[1,4,48]{1,0,2:T(2,128)(2,1)S(1)} %copy.292), channel_id=12, replica_groups=mesh['shard'=16,'context'=4,'tensor'=2] {'shard'}, dimensions={2}, use_global_device_ids=true | all-gather | bytes 6528 | tf_op jit(solution)/shard_map/all_gather | solution.py:79
  370.8 24.5 %all-gather.14 = bf16[1,384,768]{1,2,0:T(8,128)(2,1)} all-gather(bf16[1,384,48]{1,2,0:T(8,128)(2,1)S(1)} %get-tuple-element.104), channel_id=16, replica_groups=mesh['shard'=16,'context'=4,'tensor'=2] {'shard'}, dimensions={2}, use_global_device_ids=true | all-gather | bytes 626688 | tf_op jit(solution)/shard_map/all_gather | solution.py:74
  460.8 22.6 %all-gather.16 = bf16[1,24,64]{1,0,2:T(2,128)(2,1)S(1)} all-gather(bf16[1,24,4]{1,0,2:T(2,128)(2,1)S(1)} %copy.294), channel_id=18, replica_groups=mesh['shard'=16,'context'=4,'tensor'=2] {'shard'}, dimensions={2}, use_global_device_ids=true | all-gather | bytes 3264 | tf_op jit(solution)/shard_map/all_gather | solution.py:76
  486.8 44.9 %all-gather.33.cloned.1.call-done = bf16[1,768,1536]{2,1,0:T(8,128)(2,1)} async-done(((bf16[1,48,1536]{2,1,0:T(8,128)(2,1)}), bf16[1,768,1536]{2,1,0:T(8,128)(2,1)}) %all-gather.33.cloned.1.call-update) | async-done | bytes 2359312 | tf_op jit(solution)/shard_map/all_gather | solution.py:75
  535.4 43.8 %all-gather.35.cloned.1.call-done = bf16[1,1536,768]{1,2,0:T(8,128)(2,1)} async-done(((bf16[1,1536,48]{1,2,0:T(8,128)(2,1)}), bf16[1,1536,768]{1,2,0:T(8,128)(2,1)}) %all-gather.35.cloned.1.call-update) | async-done | bytes 2359312 | tf_op jit(solution)/shard_map/all_gather | solution.py:77
  612.0 26.7 %all-reduce.34.cloned.1.call-done = f32[2,128,768]{2,1,0:T(8,128)} async-done(((f32[2,128,768]{2,1,0:T(8,128)}), f32[2,128,768]{2,1,0:T(8,128)}) %all-reduce.34.cloned.1.call-update) | async-done | bytes 786448 | tf_op jit(solution)/shard_map/psum | solution.py:138
  679.2 24.7 %reduce-scatter.23.cloned.1.call-done = bf16[2,128,384]{2,1,0:T(8,128)(2,1)} async-done(((bf16[2,512,384]{2,1,0:T(8,128)(2,1)}), bf16[2,128,384]{2,1,0:T(8,128)(2,1)}) %reduce-scatter.23.cloned.1.call-update) | async-done | bytes 196624 | tf_op jit(solution)/shard_map/reduce_scatter | solution.py:255
  707.3 24.0 %all-reduce.38.cloned.1.call-done = bf16[2,128,768]{2,1,0:T(8,128)(2,1)} async-done(((bf16[2,128,768]{2,1,0:T(8,128)(2,1)}), bf16[2,128,768]{2,1,0:T(8,128)(2,1)}) %all-reduce.38.cloned.1.call-update) | async-done | bytes 393232 | tf_op jit(solution)/shard_map/psum | solution.py:269
  738.9 25.5 %all-reduce.40.cloned.1.call-done = bf16[2,128,768]{2,1,0:T(8,128)(2,1)} async-done(((bf16[2,128,768]{2,1,0:T(8,128)(2,1)}), bf16[2,128,768]{2,1,0:T(8,128)(2,1)}) %all-reduce.40.cloned.1.call-update) | async-done | bytes 393232 | tf_op jit(solution)/shard_map/psum | solution.py:216
  804.6 24.5 %reduce-scatter.27.cloned.1.call-done = bf16[2,128,384]{2,1,0:T(8,128)(2,1)} async-done(((bf16[2,512,384]{2,1,0:T(8,128)(2,1)}), bf16[2,128,384]{2,1,0:T(8,128)(2,1)}) %reduce-scatter.27.cloned.1.call-update) | async-done | bytes 196624 | tf_op jit(solution)/shard_map/reduce_scatter | solution.py:255
  875.5 75.6 %all-reduce.12 = (bf16[2,6,64]{1,0,2:T(2,128)(2,1)S(1)}, bf16[2,6,64]{1,0,2:T(2,128)(2,1)S(1)}, bf16[24,64]{1,0:T(8,128)(2,1)S(1)}, bf16[24,64]{1,0:T(8,128)(2,1...) all-reduce(bf16[2,6,64]{1,0,2:T(2,128)(2,1)S(1)} %copy.249, ...), channel_id=27, replica_groups=mesh['shard'=16,'context'=4,'tensor'=2] {'shard'}, use_global_device_ids=true, to_apply=%region_44.45.clone | all-reduce | flops 13824 | bytes 55296
  956.3 52.0 %reduce-scatter.37.cloned.1.call-done = bf16[384,48]{0,1:T(8,128)(2,1)} async-done(((bf16[384,768]{0,1:T(8,128)(2,1)}), bf16[384,48]{0,1:T(8,128)(2,1)}) %reduce-scatter.37.cloned.1.call-update) | async-done | bytes 36880
  1008.4 111.1 %all-reduce.44.cloned.1.call-done = (bf16[3,768,384]{2,0,1:T(4,128)(2,1)}, bf16[3,768,384]{2,0,1:T(4,128)(2,1)}) async-done(((bf16[3,768,384]{2,0,1:T(4,128)(2,1)}, bf16[3,768,384]{2,0,1:T(4,128)(2,1)}), (bf16[3,768,384]{2,0,1:T(4,128)(2,1)}, bf16[3,768,384]{2,0,1:T(4,128)(2,1)})) %all-reduce.44.cloned.1.call-update) | async-done | bytes 3538960
  1122.7 75.1 %reduce-scatter.31.cloned.1.call-done = bf16[48,1536]{1,0:T(8,128)(2,1)} async-done(((bf16[768,1536]{1,0:T(8,128)(2,1)}), bf16[48,1536]{1,0:T(8,128)(2,1)}) %reduce-scatter.31.cloned.1.call-update) | async-done | bytes 147472 | tf_op jit(solution)/shard_map/reduce_scatter | solution.py:305
  1197.8 77.9 %reduce-scatter.35.cloned.1.call-done = bf16[1536,48]{0,1:T(8,128)(2,1)} async-done(((bf16[1536,768]{0,1:T(8,128)(2,1)}), bf16[1536,48]{0,1:T(8,128)(2,1)}) %reduce-scatter.35.cloned.1.call-update) | async-done | bytes 147472 | tf_op jit(solution)/shard_map/reduce_scatter | solution.py:317
  1275.7 77.7 %reduce-scatter.29.cloned.1.call-done = bf16[48,1536]{1,0:T(8,128)(2,1)} async-done(((bf16[768,1536]{1,0:T(8,128)(2,1)}), bf16[48,1536]{1,0:T(8,128)(2,1)}) %reduce-scatter.29.cloned.1.call-update) | async-done | bytes 147472 | tf_op jit(solution)/shard_map/reduce_scatter | solution.py:305
  1353.3 77.9 %reduce-scatter.33.cloned.1.call-done = bf16[1536,48]{0,1:T(8,128)(2,1)} async-done(((bf16[1536,768]{0,1:T(8,128)(2,1)}), bf16[1536,48]{0,1:T(8,128)(2,1)}) %reduce-scatter.33.cloned.1.call-update) | async-done | bytes 147472 | tf_op jit(solution)/shard_map/reduce_scatter | solution.py:317
  1432.5 43.3 %all-reduce.46.cloned.1.call-done = (bf16[1,2,6,4]{2,3,1,0:T(4,128)(2,1)}, bf16[1,2,6,4]{2,3,1,0:T(4,128)(2,1)}, bf16[1,384,48]{1,2,0:T(8,128)(2,1)}, bf16[1,384...) async-done(((bf16[1,2,6,4]{2,3,1,0:T(4,128)(2,1)}, ...) | async-done | bytes 75472 | tf_op jit(solution)/shard_map/psum | solution.py:292
  1482.4 42.9 %all-reduce.48.cloned.1.call-done = (bf16[1,3,48,384]{3,1,2,0:T(4,128)(2,1)}, bf16[1,3,48,384]{3,1,2,0:T(4,128)(2,1)}, bf16[1,48,1536]{2,1,0:T(8,128)(2,1)}, bf1...) async-done(((bf16[1,3,48,384]{3,1,2,0:T(4,128)(2,1)}, bf16[1,3,48,384]{3,1,2,0:T(4,128)(2,1)}, bf16[1,48,1536]{2,1,0:T(8,128)(2,1)}, ...) | async-done | bytes 811024 | tf_op jit(solution)/shard_map/psum | solution.py:286
  (449 shorter events, 438.4 us)
Async XLA Ops:
  7.2 126.0 %all-gather.25.cloned.1.call-start = ((), (), s32[]{:S(2)}) async-start(), calls=%async_computation.26 | async-start | bytes 1880064 | tf_op jit(solution)/shard_map/all_gather | solution.py:72
  9.0 190.7 %all-reduce.28.cloned.1.call-start = ((), (), s32[]{:S(2)}) async-start(), calls=%async_computation.10 | async-start | bytes 1572864 | tf_op jit(solution)/shard_map/psum | solution.py:128
  176.1 72.3 %all-gather.27.cloned.1.call-start = ((), (), s32[]{:S(2)}) async-start(), calls=%async_computation.27 | async-start | bytes 2506752 | tf_op jit(solution)/shard_map/all_gather | solution.py:75
  176.9 119.4 %all-gather.29.cloned.1.call-start = ((), (), s32[]{:S(2)}) async-start(), calls=%async_computation.28 | async-start | bytes 2506752 | tf_op jit(solution)/shard_map/all_gather | solution.py:77
  177.7 233.5 %all-reduce.30.cloned.1.call-start = ((), (), s32[]{:S(2)}) async-start(), calls=%async_computation.11 | async-start | bytes 1572864 | tf_op jit(solution)/shard_map/psum | solution.py:138
  299.9 112.8 %all-gather.31.cloned.1.call-start = ((), (), s32[]{:S(2)}) async-start(), calls=%async_computation.29 | async-start | bytes 1880064 | tf_op jit(solution)/shard_map/all_gather | solution.py:72
  300.5 183.7 %all-reduce.32.cloned.1.call-start = ((), (), s32[]{:S(2)}) async-start(), calls=%async_computation.12 | async-start | bytes 1572864 | tf_op jit(solution)/shard_map/psum | solution.py:128
  459.3 72.4 %all-gather.33.cloned.1.call-start = ((), (), s32[]{:S(2)}) async-start(), calls=%async_computation.30 | async-start | bytes 2506752 | tf_op jit(solution)/shard_map/all_gather | solution.py:75
  460.0 119.1 %all-gather.35.cloned.1.call-start = ((), (), s32[]{:S(2)}) async-start(), calls=%async_computation.31 | async-start | bytes 2506752 | tf_op jit(solution)/shard_map/all_gather | solution.py:77
  460.7 148.8 %all-reduce.36.cloned.1.call-start = ((), (), s32[]{:S(2)}) async-start(), calls=%async_computation.14 | async-start | bytes 786432 | tf_op jit(solution)/shard_map/psum | solution.py:216
  590.2 89.0 %reduce-scatter.21.cloned.1.call-start = ((), (), s32[]{:S(2)}) async-start(), calls=%async_computation.15 | async-start | bytes 983040 | tf_op jit(solution)/shard_map/reduce_scatter | solution.py:252
  661.4 69.9 %all-reduce.38.cloned.1.call-start = ((), (), s32[]{:S(2)}) async-start(), calls=%async_computation.17 | async-start | bytes 786432 | tf_op jit(solution)/shard_map/psum | solution.py:269
  707.2 57.2 %all-reduce.40.cloned.1.call-start = ((), (), s32[]{:S(2)}) async-start(), calls=%async_computation.18 | async-start | bytes 786432 | tf_op jit(solution)/shard_map/psum | solution.py:216
  738.9 65.7 %reduce-scatter.25.cloned.1.call-start = ((), (), s32[]{:S(2)}) async-start(), calls=%async_computation.19 | async-start | bytes 983040 | tf_op jit(solution)/shard_map/reduce_scatter | solution.py:252
  787.0 85.9 %all-reduce.42.cloned.1.call-start = ((), (), s32[]{:S(2)}) async-start(), calls=%async_computation.21 | async-start | bytes 786432 | tf_op jit(solution)/shard_map/psum | solution.py:269
  832.3 123.9 %reduce-scatter.39.cloned.1.call-start = ((), (), s32[]{:S(2)}) async-start(), calls=%async_computation.33 | async-start | bytes 626688
  834.9 173.4 %reduce-scatter.37.cloned.1.call-start = ((), (), s32[]{:S(2)}) async-start(), calls=%async_computation.32 | async-start | bytes 626688
  837.3 282.1 %all-reduce.44.cloned.1.call-start = ((), (), s32[]{:S(2)}) async-start(), calls=%async_computation.34 | async-start | bytes 9437184
  853.1 344.7 %reduce-scatter.31.cloned.1.call-start = ((), (), s32[]{:S(2)}) async-start(), calls=%async_computation.23 | async-start | bytes 2506752 | tf_op jit(solution)/shard_map/reduce_scatter | solution.py:305
  856.6 419.0 %reduce-scatter.35.cloned.1.call-start = ((), (), s32[]{:S(2)}) async-start(), calls=%async_computation.25 | async-start | bytes 2506752 | tf_op jit(solution)/shard_map/reduce_scatter | solution.py:317
  861.6 491.7 %reduce-scatter.29.cloned.1.call-start = ((), (), s32[]{:S(2)}) async-start(), calls=%async_computation.22 | async-start | bytes 2506752 | tf_op jit(solution)/shard_map/reduce_scatter | solution.py:305
  865.1 566.1 %reduce-scatter.33.cloned.1.call-start = ((), (), s32[]{:S(2)}) async-start(), calls=%async_computation.24 | async-start | bytes 2506752 | tf_op jit(solution)/shard_map/reduce_scatter | solution.py:317
  869.2 606.6 %all-reduce.46.cloned.1.call-start = ((), (), s32[]{:S(2)}) async-start(), calls=%async_computation.35 | async-start | bytes 165888 | tf_op jit(solution)/shard_map/psum | solution.py:292
  1008.3 516.9 %all-reduce.48.cloned.1.call-start = ((), (), s32[]{:S(2)}) async-start(), calls=%async_computation.36 | async-start | bytes 1769472 | tf_op jit(solution)/shard_map/psum | solution.py:286
  (96 other events, 2521.8 us)
Sparse Core Ops, SparseCore 0:
  10.8 47.1 all-gather.24
  201.2 47.1 all-gather.26
  251.2 45.0 all-gather.28
  300.0 24.0 all-reduce.29
  326.1 46.5 all-gather.30
  484.5 47.1 all-gather.32
  534.0 45.0 all-gather.34
  586.2 23.2 all-reduce.35
  612.5 26.1 all-reduce.33
  655.4 23.8 reduce-scatter.20
  681.8 22.1 reduce-scatter.22
  707.4 23.8 all-reduce.37
  739.0 25.3 all-reduce.39
  780.6 23.8 reduce-scatter.24
  832.5 23.8 all-reduce.41
  860.1 73.2 reduce-scatter.38
  937.1 71.1 reduce-scatter.36
  1011.7 107.6 all-reduce.43
  1123.1 74.6 reduce-scatter.30
  1201.4 74.1 reduce-scatter.34
  1279.2 74.1 reduce-scatter.28
  1357.0 74.2 reduce-scatter.32
  1435.6 40.1 all-reduce.45
  1479.0 46.2 all-reduce.47
  (3 shorter events, 66.0 us)
where the time goes:
time: 1540 us
  waiting for transfers between devices  913 us (59%)
  blocking collectives  373 us (24%)
  local copies, waits for them, and re-layouts  101 us (7%)
  matrix products  92.7 us (6%)
  other arithmetic  40.6 us (3%)
  between operations  17.3 us (1%)
    unnamed x30, waiting for transfers between devices  165 us
    reduce_scatter x2, waiting for transfers between devices, per_device(): lax.psum_scatter(grad_parts[5].astype(jnp.bfloat16), 'shard', scatter_dim...  156 us
    reduce_scatter x2, waiting for transfers between devices, per_device(): lax.psum_scatter(grad_parts[3].astype(jnp.bfloat16), 'shard', scatter_dim...  153 us
    all_gather x2, waiting for transfers between devices, per_device(): lax.all_gather(expansion[layer_index], 'shard', axis=0, tiled=True)  91.9 us
    all_gather x2, waiting for transfers between devices, per_device(): lax.all_gather(contraction[layer_index], 'shard', axis=1, tiled=True)  89.1 us
    unnamed x1, blocking collectives  75.6 us
    reduce_scatter x2, waiting for transfers between devices, per_device(): lax.psum_scatter(value_full.astype(jnp.bfloat16), 'context', scatter_dime...  49.3 us
    all_gather x2, blocking collectives, per_device(): lax.all_gather(offsets[layer_index], 'shard', axis=1, tiled=True)  48.7 us
  transfers between devices with their start and end apart: 27, of which 20 were waited for; matrix products, arithmetic and copies ran while one was open for 9% of the time, Pallas kernels for 0%

commit v1 on v0

--- a/solution.py
+++ b/solution.py
@@ -8,6 +8,12 @@
 GELU_COEF = 0.7978845608028654
 GELU_CUBE = 0.044715
 MASKED = -1e30
+
+
+def gather_by_exchange(x, axis, dim):
+    size = lax.axis_size(axis)
+    repeats = [size if d == dim else 1 for d in range(x.ndim)]
+    return lax.all_to_all(jnp.tile(x, repeats), axis, split_axis=dim, concat_axis=dim, tiled=True)
 
 
 def gelu_value(preact):
@@ -71,7 +77,7 @@
         weights = (
             lax.all_gather(projection[layer_index], "shard", axis=1, tiled=True),
             lax.all_gather(head_bias[layer_index], "shard", axis=2, tiled=True),
-            lax.all_gather(mixing[layer_index], "shard", axis=1, tiled=True),
+            gather_by_exchange(mixing[layer_index], "shard", 1),
             lax.all_gather(expansion[layer_index], "shard", axis=0, tiled=True),
             lax.all_gather(hidden_bias[layer_index], "shard", axis=1, tiled=True),
             lax.all_gather(contraction[layer_index], "shard", axis=1, tiled=True),

time: 1540 us -> 1520 us (0.987)
  waiting for transfers between devices: 913 us -> 860 us
    psum x2, waiting for transfers between devices: 44.5 us -> 0.01 us  [per_device(): lax.psum(feed_partial.astype(jnp.bfloat16), 'tensor').astype(jnp.float32)]
  transfers between devices with their start and end apart: 27 -> 29, of which waited for: 20 -> 18; matrix products, arithmetic and copies ran while one was open for 9% -> 11% of each run, Pallas kernels for 0% -> 0%
where the time goes in v1:
time: 1520 us; the launch traced here: 1510 us
  waiting for transfers between devices  860 us (57%)
  blocking collectives  381 us (25%)
  local copies, waits for them, and re-layouts  105 us (7%)
  matrix products  93.1 us (6%)
  other arithmetic  42.1 us (3%)
  between operations  17.3 us (1%)
    unnamed x30, waiting for transfers between devices  165 us
    reduce_scatter x2, waiting for transfers between devices, per_device(): lax.psum_scatter(grad_parts[5].astype(jnp.bfloat16), 'shard', scatter_dim...  156 us
    reduce_scatter x2, waiting for transfers between devices, per_device(): lax.psum_scatter(grad_parts[3].astype(jnp.bfloat16), 'shard', scatter_dim...  153 us
    all_gather x2, waiting for transfers between devices, per_device(): lax.all_gather(expansion[layer_index], 'shard', axis=0, tiled=True)  93.6 us
    all_gather x2, waiting for transfers between devices, per_device(): lax.all_gather(contraction[layer_index], 'shard', axis=1, tiled=True)  88 us
    unnamed x1, blocking collectives  75.5 us
    all_gather x2, blocking collectives, per_device(): lax.all_gather(offsets[layer_index], 'shard', axis=1, tiled=True)  53 us
    all_gather x2, blocking collectives, per_device(): lax.all_gather(mixing[layer_index], 'shard', axis=1, tiled=True)  52.7 us
  transfers between devices with their start and end apart: 29, of which 18 were waited for; matrix products, arithmetic and copies ran while one was open for 11% of the time, Pallas kernels for 0%

profile of v1, /device:TPU:0, one launch (start us, length us, event | category | flops | bytes accessed | tf_op | source)
XLA Modules:
  0.0 1512.7 jit_solution(6753785413496350685)
XLA Ops:
  20.1 26.9 %all-gather.1 = bf16[1,4,768]{1,0,2:T(2,128)(2,1)S(1)} all-gather(bf16[1,4,48]{1,0,2:T(2,128)(2,1)S(1)} %copy.302), channel_id=3, replica_groups=mesh['shard'=16,'context'=4,'tensor'=2] {'shard'}, dimensions={2}, use_global_device_ids=true | all-gather | bytes 6528 | tf_op jit(solution)/shard_map/all_gather | solution.py:85
  70.5 22.3 %all-gather.3 = bf16[1,2,6,64]{2,1,0,3:T(2,128)(2,1)S(1)} all-gather(bf16[1,2,6,4]{2,1,0,3:T(2,128)(2,1)S(1)} %copy.303), channel_id=5, replica_groups=mesh['shard'=16,'context'=4,'tensor'=2] {'shard'}, dimensions={3}, use_global_device_ids=true | all-gather | bytes 1632 | tf_op jit(solution)/shard_map/all_gather | solution.py:79
  162.8 22.2 %all-gather.6 = bf16[1,24,64]{1,0,2:T(2,128)(2,1)S(1)} all-gather(bf16[1,24,4]{1,0,2:T(2,128)(2,1)S(1)} %copy.304), channel_id=8, replica_groups=mesh['shard'=16,'context'=4,'tensor'=2] {'shard'}, dimensions={2}, use_global_device_ids=true | all-gather | bytes 3264 | tf_op jit(solution)/shard_map/all_gather | solution.py:82
  186.8 46.4 %all-gather.27.cloned.1.call-done = bf16[1,768,1536]{2,1,0:T(8,128)(2,1)} async-done(((bf16[1,48,1536]{2,1,0:T(8,128)(2,1)}), bf16[1,768,1536]{2,1,0:T(8,128)(2,1)}) %all-gather.27.cloned.1.call-update) | async-done | bytes 2359312 | tf_op jit(solution)/shard_map/all_gather | solution.py:81
  236.9 44.2 %all-gather.29.cloned.1.call-done = bf16[1,1536,768]{1,2,0:T(8,128)(2,1)} async-done(((bf16[1,1536,48]{1,2,0:T(8,128)(2,1)}), bf16[1,1536,768]{1,2,0:T(8,128)(2,1)}) %all-gather.29.cloned.1.call-update) | async-done | bytes 2359312 | tf_op jit(solution)/shard_map/all_gather | solution.py:83
  291.8 26.1 %all-gather.9 = bf16[1,4,768]{1,0,2:T(2,128)(2,1)S(1)} all-gather(bf16[1,4,48]{1,0,2:T(2,128)(2,1)S(1)} %copy.306), channel_id=11, replica_groups=mesh['shard'=16,'context'=4,'tensor'=2] {'shard'}, dimensions={2}, use_global_device_ids=true | all-gather | bytes 6528 | tf_op jit(solution)/shard_map/all_gather | solution.py:85
  318.5 22.5 %all-gather.8 = bf16[1,2,768]{1,0,2:T(2,128)(2,1)S(1)} all-gather(bf16[1,2,48]{1,0,2:T(2,128)(2,1)S(1)} %copy.305), channel_id=10, replica_groups=mesh['shard'=16,'context'=4,'tensor'=2] {'shard'}, dimensions={2}, use_global_device_ids=true | all-gather | bytes 3264 | tf_op jit(solution)/shard_map/all_gather | solution.py:84
  341.4 22.2 %all-gather.11 = bf16[1,2,6,64]{2,1,0,3:T(2,128)(2,1)S(1)} all-gather(bf16[1,2,6,4]{2,1,0,3:T(2,128)(2,1)S(1)} %copy.307), channel_id=13, replica_groups=mesh['shard'=16,'context'=4,'tensor'=2] {'shard'}, dimensions={3}, use_global_device_ids=true | all-gather | bytes 1632 | tf_op jit(solution)/shard_map/all_gather | solution.py:79
  456.2 47.1 %all-gather.33.cloned.1.call-done = bf16[1,768,1536]{2,1,0:T(8,128)(2,1)} async-done(((bf16[1,48,1536]{2,1,0:T(8,128)(2,1)}), bf16[1,768,1536]{2,1,0:T(8,128)(2,1)}) %all-gather.33.cloned.1.call-update) | async-done | bytes 2359312 | tf_op jit(solution)/shard_map/all_gather | solution.py:81
  507.1 43.8 %all-gather.35.cloned.1.call-done = bf16[1,1536,768]{1,2,0:T(8,128)(2,1)} async-done(((bf16[1,1536,48]{1,2,0:T(8,128)(2,1)}), bf16[1,1536,768]{1,2,0:T(8,128)(2,1)}) %all-gather.35.cloned.1.call-update) | async-done | bytes 2359312 | tf_op jit(solution)/shard_map/all_gather | solution.py:83
  562.0 25.5 %all-gather.16 = bf16[1,384,768]{1,2,0:T(8,128)(2,1)} all-gather(bf16[1,384,48]{1,2,0:T(8,128)(2,1)} %get-tuple-element.107), channel_id=18, replica_groups=mesh['shard'=16,'context'=4,'tensor'=2] {'shard'}, dimensions={2}, use_global_device_ids=true | all-gather | bytes 626688 | tf_op jit(solution)/shard_map/all_gather | solution.py:188
  650.9 24.8 %reduce-scatter.23.cloned.1.call-done = bf16[2,128,384]{2,1,0:T(8,128)(2,1)} async-done(((bf16[2,512,384]{2,1,0:T(8,128)(2,1)}), bf16[2,128,384]{2,1,0:T(8,128)(2,1)}) %reduce-scatter.23.cloned.1.call-update) | async-done | bytes 196624 | tf_op jit(solution)/shard_map/reduce_scatter | solution.py:261
  679.0 23.9 %all-reduce.38.cloned.1.call-done = bf16[2,128,768]{2,1,0:T(8,128)(2,1)} async-done(((bf16[2,128,768]{2,1,0:T(8,128)(2,1)}), bf16[2,128,768]{2,1,0:T(8,128)(2,1)}) %all-reduce.38.cloned.1.call-update) | async-done | bytes 393232 | tf_op jit(solution)/shard_map/psum | solution.py:275
  711.7 27.2 %all-gather.17 = bf16[1,384,768]{1,2,0:T(8,128)(2,1)} all-gather(bf16[1,384,48]{1,2,0:T(8,128)(2,1)} %get-tuple-element.104), channel_id=19, replica_groups=mesh['shard'=16,'context'=4,'tensor'=2] {'shard'}, dimensions={2}, use_global_device_ids=true | all-gather | bytes 626688 | tf_op jit(solution)/shard_map/all_gather | solution.py:188
  778.4 24.6 %reduce-scatter.27.cloned.1.call-done = bf16[2,128,384]{2,1,0:T(8,128)(2,1)} async-done(((bf16[2,512,384]{2,1,0:T(8,128)(2,1)}), bf16[2,128,384]{2,1,0:T(8,128)(2,1)}) %reduce-scatter.27.cloned.1.call-update) | async-done | bytes 196624 | tf_op jit(solution)/shard_map/reduce_scatter | solution.py:261
  850.2 75.5 %all-reduce.12 = (bf16[2,6,64]{1,0,2:T(2,128)(2,1)S(1)}, bf16[2,6,64]{1,0,2:T(2,128)(2,1)S(1)}, bf16[24,64]{1,0:T(8,128)(2,1)S(1)}, bf16[24,64]{1,0:T(8,128)(2,1...) all-reduce(bf16[2,6,64]{1,0,2:T(2,128)(2,1)S(1)} %copy.259, ...), channel_id=27, replica_groups=mesh['shard'=16,'context'=4,'tensor'=2] {'shard'}, use_global_device_ids=true, to_apply=%region_44.45.clone | all-reduce | flops 13824 | bytes 55296
  930.9 51.5 %reduce-scatter.37.cloned.1.call-done = bf16[384,48]{0,1:T(8,128)(2,1)} async-done(((bf16[384,768]{0,1:T(8,128)(2,1)}), bf16[384,48]{0,1:T(8,128)(2,1)}) %reduce-scatter.37.cloned.1.call-update) | async-done | bytes 36880
  982.4 111.1 %all-reduce.44.cloned.1.call-done = (bf16[3,768,384]{2,0,1:T(4,128)(2,1)}, bf16[3,768,384]{2,0,1:T(4,128)(2,1)}) async-done(((bf16[3,768,384]{2,0,1:T(4,128)(2,1)}, bf16[3,768,384]{2,0,1:T(4,128)(2,1)}), (bf16[3,768,384]{2,0,1:T(4,128)(2,1)}, bf16[3,768,384]{2,0,1:T(4,128)(2,1)})) %all-reduce.44.cloned.1.call-update) | async-done | bytes 3538960
  1096.7 75.1 %reduce-scatter.31.cloned.1.call-done = bf16[48,1536]{1,0:T(8,128)(2,1)} async-done(((bf16[768,1536]{1,0:T(8,128)(2,1)}), bf16[48,1536]{1,0:T(8,128)(2,1)}) %reduce-scatter.31.cloned.1.call-update) | async-done | bytes 147472 | tf_op jit(solution)/shard_map/reduce_scatter | solution.py:311
  1171.8 77.9 %reduce-scatter.35.cloned.1.call-done = bf16[1536,48]{0,1:T(8,128)(2,1)} async-done(((bf16[1536,768]{0,1:T(8,128)(2,1)}), bf16[1536,48]{0,1:T(8,128)(2,1)}) %reduce-scatter.35.cloned.1.call-update) | async-done | bytes 147472 | tf_op jit(solution)/shard_map/reduce_scatter | solution.py:323
  1249.7 77.7 %reduce-scatter.29.cloned.1.call-done = bf16[48,1536]{1,0:T(8,128)(2,1)} async-done(((bf16[768,1536]{1,0:T(8,128)(2,1)}), bf16[48,1536]{1,0:T(8,128)(2,1)}) %reduce-scatter.29.cloned.1.call-update) | async-done | bytes 147472 | tf_op jit(solution)/shard_map/reduce_scatter | solution.py:311
  1327.4 77.9 %reduce-scatter.33.cloned.1.call-done = bf16[1536,48]{0,1:T(8,128)(2,1)} async-done(((bf16[1536,768]{0,1:T(8,128)(2,1)}), bf16[1536,48]{0,1:T(8,128)(2,1)}) %reduce-scatter.33.cloned.1.call-update) | async-done | bytes 147472 | tf_op jit(solution)/shard_map/reduce_scatter | solution.py:323
  1406.5 43.3 %all-reduce.46.cloned.1.call-done = (bf16[1,2,6,4]{2,3,1,0:T(4,128)(2,1)}, bf16[1,2,6,4]{2,3,1,0:T(4,128)(2,1)}, bf16[1,384,48]{1,2,0:T(8,128)(2,1)}, bf16[1,384...) async-done(((bf16[1,2,6,4]{2,3,1,0:T(4,128)(2,1)}, ...) | async-done | bytes 75472 | tf_op jit(solution)/shard_map/psum | solution.py:298
  1456.4 42.9 %all-reduce.48.cloned.1.call-done = (bf16[1,3,48,384]{3,1,2,0:T(4,128)(2,1)}, bf16[1,3,48,384]{3,1,2,0:T(4,128)(2,1)}, bf16[1,48,1536]{2,1,0:T(8,128)(2,1)}, bf1...) async-done(((bf16[1,3,48,384]{3,1,2,0:T(4,128)(2,1)}, bf16[1,3,48,384]{3,1,2,0:T(4,128)(2,1)}, bf16[1,48,1536]{2,1,0:T(8,128)(2,1)}, ...) | async-done | bytes 811024 | tf_op jit(solution)/shard_map/psum | solution.py:292
  (451 shorter events, 412.9 us)
Async XLA Ops:
  7.2 112.7 %all-gather.25.cloned.1.call-start = ((), (), s32[]{:S(2)}) async-start(), calls=%async_computation.28 | async-start | bytes 1880064 | tf_op jit(solution)/shard_map/all_gather | solution.py:78
  11.2 146.9 %all-to-all-start = ((bf16[384,16,48]{0,2,1:T(8,128)(2,1)}), bf16[384,16,48]{0,2,1:T(8,128)(2,1)}, u32[]{:S(2)}, u32[]{:S(2)}) async-start(bf16[384,16,48]{0,2,1:T(8,128)(2,1)} %tile.17), calls=%async_computation | async-start | bytes 1179648 | tf_op jit(solution)/shard_map/all_to_all | solution.py:16
  19.3 165.9 %all-reduce.28.cloned.1.call-start = ((), (), s32[]{:S(2)}) async-start(), calls=%async_computation.12 | async-start | bytes 1572864 | tf_op jit(solution)/shard_map/psum | solution.py:134
  160.6 72.7 %all-gather.27.cloned.1.call-start = ((), (), s32[]{:S(2)}) async-start(), calls=%async_computation.29 | async-start | bytes 2506752 | tf_op jit(solution)/shard_map/all_gather | solution.py:81
  161.4 119.8 %all-gather.29.cloned.1.call-start = ((), (), s32[]{:S(2)}) async-start(), calls=%async_computation.30 | async-start | bytes 2506752 | tf_op jit(solution)/shard_map/all_gather | solution.py:83
  162.2 218.6 %all-reduce.30.cloned.1.call-start = ((), (), s32[]{:S(2)}) async-start(), calls=%async_computation.13 | async-start | bytes 1572864 | tf_op jit(solution)/shard_map/psum | solution.py:144
  285.2 97.1 %all-gather.31.cloned.1.call-start = ((), (), s32[]{:S(2)}) async-start(), calls=%async_computation.31 | async-start | bytes 1880064 | tf_op jit(solution)/shard_map/all_gather | solution.py:78
  286.7 140.7 %all-to-all-start.1 = ((bf16[384,16,48]{0,2,1:T(8,128)(2,1)}), bf16[384,16,48]{0,2,1:T(8,128)(2,1)}, u32[]{:S(2)}, u32[]{:S(2)}) async-start(bf16[384,16,48]{0,2,1:T(8,128)(2,1)} %tile.19), calls=%async_computation.1 | async-start | bytes 1179648 | tf_op jit(solution)/shard_map/all_to_all | solution.py:16
  291.7 161.9 %all-reduce.32.cloned.1.call-start = ((), (), s32[]{:S(2)}) async-start(), calls=%async_computation.14 | async-start | bytes 1572864 | tf_op jit(solution)/shard_map/psum | solution.py:134
  429.8 73.6 %all-gather.33.cloned.1.call-start = ((), (), s32[]{:S(2)}) async-start(), calls=%async_computation.32 | async-start | bytes 2506752 | tf_op jit(solution)/shard_map/all_gather | solution.py:81
  430.6 120.3 %all-gather.35.cloned.1.call-start = ((), (), s32[]{:S(2)}) async-start(), calls=%async_computation.33 | async-start | bytes 2506752 | tf_op jit(solution)/shard_map/all_gather | solution.py:83
  431.3 156.2 %all-reduce.36.cloned.1.call-start = ((), (), s32[]{:S(2)}) async-start(), calls=%async_computation.16 | async-start | bytes 786432 | tf_op jit(solution)/shard_map/psum | solution.py:222
  561.9 89.0 %reduce-scatter.21.cloned.1.call-start = ((), (), s32[]{:S(2)}) async-start(), calls=%async_computation.17 | async-start | bytes 983040 | tf_op jit(solution)/shard_map/reduce_scatter | solution.py:258
  633.1 69.9 %all-reduce.38.cloned.1.call-start = ((), (), s32[]{:S(2)}) async-start(), calls=%async_computation.19 | async-start | bytes 786432 | tf_op jit(solution)/shard_map/psum | solution.py:275
  762.3 85.3 %all-reduce.42.cloned.1.call-start = ((), (), s32[]{:S(2)}) async-start(), calls=%async_computation.23 | async-start | bytes 786432 | tf_op jit(solution)/shard_map/psum | solution.py:275
  806.4 124.4 %reduce-scatter.39.cloned.1.call-start = ((), (), s32[]{:S(2)}) async-start(), calls=%async_computation.35 | async-start | bytes 626688
  808.9 173.4 %reduce-scatter.37.cloned.1.call-start = ((), (), s32[]{:S(2)}) async-start(), calls=%async_computation.34 | async-start | bytes 626688
  811.4 282.1 %all-reduce.44.cloned.1.call-start = ((), (), s32[]{:S(2)}) async-start(), calls=%async_computation.36 | async-start | bytes 9437184
  827.0 344.8 %reduce-scatter.31.cloned.1.call-start = ((), (), s32[]{:S(2)}) async-start(), calls=%async_computation.25 | async-start | bytes 2506752 | tf_op jit(solution)/shard_map/reduce_scatter | solution.py:311
  831.2 418.4 %reduce-scatter.35.cloned.1.call-start = ((), (), s32[]{:S(2)}) async-start(), calls=%async_computation.27 | async-start | bytes 2506752 | tf_op jit(solution)/shard_map/reduce_scatter | solution.py:323
  836.2 491.1 %reduce-scatter.29.cloned.1.call-start = ((), (), s32[]{:S(2)}) async-start(), calls=%async_computation.24 | async-start | bytes 2506752 | tf_op jit(solution)/shard_map/reduce_scatter | solution.py:311
  839.7 565.6 %reduce-scatter.33.cloned.1.call-start = ((), (), s32[]{:S(2)}) async-start(), calls=%async_computation.26 | async-start | bytes 2506752 | tf_op jit(solution)/shard_map/reduce_scatter | solution.py:323
  843.9 605.9 %all-reduce.46.cloned.1.call-start = ((), (), s32[]{:S(2)}) async-start(), calls=%async_computation.37 | async-start | bytes 165888 | tf_op jit(solution)/shard_map/psum | solution.py:298
  982.3 516.9 %all-reduce.48.cloned.1.call-start = ((), (), s32[]{:S(2)}) async-start(), calls=%async_computation.38 | async-start | bytes 1769472 | tf_op jit(solution)/shard_map/psum | solution.py:292
  (96 other events, 2294.0 us)
Sparse Core Ops, SparseCore 0:
  10.8 48.6 all-gather.24
  160.7 22.3 all-reduce.27
  186.0 47.1 all-gather.26
  236.0 45.0 all-gather.28
  285.4 24.0 all-reduce.29
  312.0 45.8 all-gather.30
  429.9 23.2 all-reduce.31
  456.2 47.1 all-gather.32
  505.7 45.0 all-gather.34
  557.9 23.2 all-reduce.35
  584.2 26.1 all-reduce.33
  627.1 23.7 reduce-scatter.20
  679.1 23.8 all-reduce.37
  711.8 25.3 all-reduce.39
  806.5 23.8 all-reduce.41
  834.2 73.2 reduce-scatter.38
  911.1 71.1 reduce-scatter.36
  985.8 107.6 all-reduce.43
  1097.1 74.6 reduce-scatter.30
  1175.5 74.1 reduce-scatter.34
  1253.2 74.1 reduce-scatter.28
  1331.0 74.2 reduce-scatter.32
  1409.6 40.1 all-reduce.45
  1453.0 46.2 all-reduce.47
  (3 shorter events, 66.4 us)
